TPU v7x, 32 devices: a whole 2x2x4 slice. The times are simulated.
32 devices in a mesh: shard: 4 (over x, core), replica: 8 (over z, y).
Axes of the slice: x: 2, y: 2, z: 4, core: 2. Of those that a mesh axis runs over, the one named last changes fastest.
Arguments:
- layer_input: bfloat16 [8192, 1600], P(('shard', 'replica')), may hold values from -6 to 6
- norm1_gain: bfloat16 [1600], P('shard'), may hold values from 0.5 to 1.5
- norm1_shift: bfloat16 [1600], P('shard'), may hold values from -3 to 3
- qkv_weight: bfloat16 [1600, 4800], P('shard')
- query_bias: bfloat16 [1600], P('shard'), may hold values from -3 to 3
- value_bias: bfloat16 [1600], P('shard'), may hold values from -3 to 3
- out_weight: bfloat16 [1600, 1600], P('shard'), may hold values from -0.625 to 0.625
- out_bias: bfloat16 [1600], P('shard'), may hold values from -3 to 3
- norm2_gain: bfloat16 [1600], P('shard'), may hold values from 0.5 to 1.5
- norm2_shift: bfloat16 [1600], P('shard'), may hold values from -3 to 3
- fc_weight: bfloat16 [1600, 6400], P('shard'), may hold values from -0.15625 to 0.15625
- fc_bias: bfloat16 [6400], P('shard'), may hold values from -3 to 3
- proj_weight: bfloat16 [6400, 1600], P('shard'), may hold values from -0.078125 to 0.078125
- proj_bias: bfloat16 [1600], P('shard'), may hold values from -3 to 3
- cotangent: bfloat16 [8192, 1600], P(('shard', 'replica')), may hold values from -6 to 6
- seq_lengths: int32 [128], replicated, may hold values from 0 to 256, as said below
- seq_device: int32 [128], replicated, may hold values from 0 to 31, as said below
- seq_offset: int32 [128], replicated, may hold values from 0 to 256, as said below
Outputs:
- output: bfloat16 [8192, 1600], P(('shard', 'replica'))
- grad_x: bfloat16 [8192, 1600], P(('shard', 'replica'))
- grad_norm1_gain: float32 [1600], P('shard')
- grad_norm1_shift: float32 [1600], P('shard')
- grad_qkv_weight: float32 [1600, 4800], P('shard')
- grad_query_bias: float32 [1600], P('shard')
- grad_value_bias: float32 [1600], P('shard')
- grad_out_weight: float32 [1600, 1600], P('shard')
- grad_out_bias: float32 [1600], P('shard')
- grad_norm2_gain: float32 [1600], P('shard')
- grad_norm2_shift: float32 [1600], P('shard')
- grad_fc_weight: float32 [1600, 6400], P('shard')
- grad_fc_bias: float32 [6400], P('shard')
- grad_proj_weight: float32 [6400, 1600], P('shard')
- grad_proj_bias: float32 [1600], P('shard')
Inputs may be any that keep to these rules, and one draw needn't show every extreme that they name: `seq_lengths`: some sequence has exactly 256 tokens; empty sequences occur. `seq_device`: device number = shard index * 8 + replica index; every device is named by exactly 4 sequences. The sequences of one device occupy disjoint ranges [seq_offset, seq_offset + seq_lengths) of its 256 positions.
All inputs are finite; a program needn't handle non-finite values.
Results may differ from a plain program's by a relative error of at most 0.018.
Values may be sent and summed in bfloat16 or wider, within the bound.
No kernel may reach another device: no remote copies, remote signals or barrier semaphores. Data moves between devices by JAX's collectives and lax.ppermute only.
A program may use at most 448 MiB of HBM per device.

v0:
```python
import math
import jax
import jax.numpy as jnp
from jax import lax
from jax.sharding import PartitionSpec as P

HEAD = 64
GELU_C = math.sqrt(2.0 / math.pi)


def normalize(values):
    centre = jnp.mean(values, axis=-1, keepdims=True)
    shifted = values - centre
    spread = jnp.mean(shifted * shifted, axis=-1, keepdims=True)
    inverse = lax.rsqrt(spread + 1e-05)
    return (shifted * inverse, inverse)


def norm_back(upstream, normed, inverse):
    first = jnp.mean(upstream, axis=-1, keepdims=True)
    second = jnp.mean(upstream * normed, axis=-1, keepdims=True)
    return inverse * (upstream - first - normed * second)


def gelu_pair(inputs):
    cubic = 0.044715 * inputs * inputs * inputs
    tangent = jnp.tanh(GELU_C * (inputs + cubic))
    value = 0.5 * inputs * (1.0 + tangent)
    slope = 0.5 * (1.0 + tangent) + 0.5 * inputs * (1.0 - tangent * tangent) * GELU_C * (
        1.0 + 3.0 * 0.044715 * inputs * inputs
    )
    return (value, slope)


def segment_ids(lengths, owners, offsets, device, count):
    position = jnp.arange(count, dtype=jnp.int32)
    number = jnp.arange(lengths.shape[0], dtype=jnp.int32)
    inside = (
        (owners[:, None] == device)
        & (position[None, :] >= offsets[:, None])
        & (position[None, :] < offsets[:, None] + lengths[:, None])
    )
    owned = jnp.sum(jnp.where(inside, number[:, None], 0), axis=0)
    filled = jnp.any(inside, axis=0)
    return (jnp.where(filled, owned, -1 - position), filled)


def product(spec, left, right):
    return jnp.einsum(spec, left, right, preferred_element_type=jnp.float32)


def mdot(left, right):
    return jnp.dot(left, right, preferred_element_type=jnp.float32)


def tdot(left, right):
    return lax.dot_general(
        left, right, (((0,), (0,)), ((), ())), preferred_element_type=jnp.float32
    )


def ndot(left, right):
    return lax.dot_general(
        left, right, (((1,), (1,)), ((), ())), preferred_element_type=jnp.float32
    )


def split_heads(packed, which):
    width_all = packed.shape[1] // 3
    return packed[:, which * width_all : (which + 1) * width_all].reshape(packed.shape[0], -1, HEAD)


def scores_of(packed, segment):
    raw = product("qhd,khd->hqk", split_heads(packed, 0), split_heads(packed, 1)) * (
        1.0 / math.sqrt(HEAD)
    )
    position = jnp.arange(packed.shape[0], dtype=jnp.int32)
    allowed = (segment[:, None] == segment[None, :]) & (position[None, :] <= position[:, None])
    return jnp.where(allowed[None], raw, -jnp.inf)


def forward(layer_input, segment, params):
    (
        gain1,
        shift1,
        w_qkv,
        b_query,
        b_value,
        w_out,
        b_out,
        gain2,
        shift2,
        w_fc,
        b_fc,
        w_proj,
        b_proj,
    ) = params
    count = layer_input.shape[0]
    inputs = layer_input.astype(jnp.float32)
    normed1, inverse1 = normalize(inputs)
    normed_in = (normed1 * gain1.astype(jnp.float32) + shift1.astype(jnp.float32)).astype(
        jnp.bfloat16
    )
    bias_all = jnp.concatenate(
        [
            b_query.astype(jnp.float32),
            jnp.zeros(b_query.shape, jnp.float32),
            b_value.astype(jnp.float32),
        ]
    )
    packed = (mdot(normed_in, w_qkv) + bias_all).astype(jnp.bfloat16)
    scores = scores_of(packed, segment)
    highest = jnp.max(scores, axis=-1, keepdims=True)
    expo = jnp.exp(scores - highest)
    total = jnp.sum(expo, axis=-1, keepdims=True)
    probs = (expo / total).astype(jnp.bfloat16)
    logsum = highest + jnp.log(total)
    mixed = (
        product("hqk,khd->qhd", probs, split_heads(packed, 2))
        .reshape(count, -1)
        .astype(jnp.bfloat16)
    )
    hidden = inputs + mdot(mixed, w_out) + b_out.astype(jnp.float32)
    normed2, inverse2 = normalize(hidden)
    mlp_in = (normed2 * gain2.astype(jnp.float32) + shift2.astype(jnp.float32)).astype(jnp.bfloat16)
    pre_act = mdot(mlp_in, w_fc) + b_fc.astype(jnp.float32)
    activ = gelu_pair(pre_act)[0].astype(jnp.bfloat16)
    result = (hidden + mdot(activ, w_proj) + b_proj.astype(jnp.float32)).astype(jnp.bfloat16)
    saved = (
        normed1,
        inverse1,
        normed_in,
        packed,
        mixed,
        logsum,
        segment,
        normed2,
        inverse2,
        mlp_in,
        pre_act,
        activ,
    )
    return (result, saved)


def attend_back(packed, grad_mixed, logsum, segment):
    count = packed.shape[0]
    scores = scores_of(packed, segment)
    back_probs = jnp.exp(scores - logsum)
    probs_low = back_probs.astype(jnp.bfloat16)
    upstream = grad_mixed.reshape(count, -1, HEAD)
    grad_values = product("hqk,qhd->khd", probs_low, upstream)
    grad_probs = product("qhd,khd->hqk", upstream, split_heads(packed, 2))
    delta = jnp.sum(back_probs * grad_probs, axis=-1, keepdims=True)
    grad_scores = (back_probs * (grad_probs - delta) * (1.0 / math.sqrt(HEAD))).astype(jnp.bfloat16)
    grad_query = product("hqk,khd->qhd", grad_scores, split_heads(packed, 1))
    grad_keys = product("hqk,qhd->khd", grad_scores, split_heads(packed, 0))
    return jnp.concatenate(
        [
            grad_query.reshape(count, -1),
            grad_keys.reshape(count, -1),
            grad_values.reshape(count, -1),
        ],
        axis=1,
    )


def backward(cotangent, filled, saved, params):
    (
        gain1,
        shift1,
        w_qkv,
        b_query,
        b_value,
        w_out,
        b_out,
        gain2,
        shift2,
        w_fc,
        b_fc,
        w_proj,
        b_proj,
    ) = params
    (
        normed1,
        inverse1,
        normed_in,
        packed,
        mixed,
        logsum,
        segment,
        normed2,
        inverse2,
        mlp_in,
        pre_act,
        activ,
    ) = saved
    upstream = jnp.where(filled[:, None], cotangent.astype(jnp.float32), 0.0)
    upstream_low = upstream.astype(jnp.bfloat16)
    grad_bproj = jnp.sum(upstream, axis=0)
    slope = gelu_pair(pre_act)[1]
    grad_pre = ndot(upstream_low, w_proj) * slope
    grad_pre_low = grad_pre.astype(jnp.bfloat16)
    grad_bfc = jnp.sum(grad_pre, axis=0)
    grad_mlp_in = ndot(grad_pre_low, w_fc)
    grad_gain2 = jnp.sum(grad_mlp_in * normed2, axis=0)
    grad_shift2 = jnp.sum(grad_mlp_in, axis=0)
    grad_hidden = upstream + norm_back(grad_mlp_in * gain2.astype(jnp.float32), normed2, inverse2)
    grad_bout = jnp.sum(grad_hidden, axis=0)
    grad_hidden_low = grad_hidden.astype(jnp.bfloat16)
    grad_mixed = ndot(grad_hidden_low, w_out).astype(jnp.bfloat16)
    grad_packed = attend_back(packed, grad_mixed, logsum, segment)
    width_all = w_out.shape[0]
    grad_bquery = jnp.sum(grad_packed[:, :width_all], axis=0)
    grad_bvalue = jnp.sum(grad_packed[:, 2 * width_all :], axis=0)
    grad_packed_low = grad_packed.astype(jnp.bfloat16)
    grad_in = ndot(grad_packed_low, w_qkv)
    grad_gain1 = jnp.sum(grad_in * normed1, axis=0)
    grad_shift1 = jnp.sum(grad_in, axis=0)
    grad_inputs = (
        grad_hidden + norm_back(grad_in * gain1.astype(jnp.float32), normed1, inverse1)
    ).astype(jnp.bfloat16)
    grad_wqkv = tdot(normed_in, grad_packed_low)
    grad_wout = tdot(mixed, grad_hidden_low)
    grad_wfc = tdot(mlp_in, grad_pre_low)
    grad_wproj = tdot(activ, upstream_low)
    grads = (
        grad_gain1,
        grad_shift1,
        grad_wqkv,
        grad_bquery,
        grad_bvalue,
        grad_wout,
        grad_bout,
        grad_gain2,
        grad_shift2,
        grad_wfc,
        grad_bfc,
        grad_wproj,
        grad_bproj,
    )
    lefts = (normed_in, mixed, mlp_in, activ)
    rights = (grad_packed_low, grad_hidden_low, grad_pre_low, upstream_low)
    return (grad_inputs, grads, lefts, rights)


def local(
    layer_input,
    norm1_gain,
    norm1_shift,
    qkv_weight,
    query_bias,
    value_bias,
    out_weight,
    out_bias,
    norm2_gain,
    norm2_shift,
    fc_weight,
    fc_bias,
    proj_weight,
    proj_bias,
    cotangent,
    seq_lengths,
    seq_device,
    seq_offset,
):
    gathered = (
        lax.all_gather(norm1_gain, "shard", axis=0, tiled=True),
        lax.all_gather(norm1_shift, "shard", axis=0, tiled=True),
        lax.all_gather(qkv_weight, "shard", axis=0, tiled=True),
        lax.all_gather(query_bias, "shard", axis=0, tiled=True),
        lax.all_gather(value_bias, "shard", axis=0, tiled=True),
        lax.all_gather(out_weight, "shard", axis=0, tiled=True),
        lax.all_gather(out_bias, "shard", axis=0, tiled=True),
        lax.all_gather(norm2_gain, "shard", axis=0, tiled=True),
        lax.all_gather(norm2_shift, "shard", axis=0, tiled=True),
        lax.all_gather(fc_weight, "shard", axis=0, tiled=True),
        lax.all_gather(fc_bias, "shard", axis=0, tiled=True),
        lax.all_gather(proj_weight, "shard", axis=0, tiled=True),
        lax.all_gather(proj_bias, "shard", axis=0, tiled=True),
    )
    device = lax.axis_index("shard") * lax.axis_size("replica") + lax.axis_index("replica")
    segment, filled = segment_ids(seq_lengths, seq_device, seq_offset, device, layer_input.shape[0])
    result, saved = forward(layer_input, segment, gathered)
    gathered = (
        lax.all_gather(norm1_gain, "shard", axis=0, tiled=True),
        lax.all_gather(norm1_shift, "shard", axis=0, tiled=True),
        lax.all_gather(qkv_weight, "shard", axis=0, tiled=True),
        lax.all_gather(query_bias, "shard", axis=0, tiled=True),
        lax.all_gather(value_bias, "shard", axis=0, tiled=True),
        lax.all_gather(out_weight, "shard", axis=0, tiled=True),
        lax.all_gather(out_bias, "shard", axis=0, tiled=True),
        lax.all_gather(norm2_gain, "shard", axis=0, tiled=True),
        lax.all_gather(norm2_shift, "shard", axis=0, tiled=True),
        lax.all_gather(fc_weight, "shard", axis=0, tiled=True),
        lax.all_gather(fc_bias, "shard", axis=0, tiled=True),
        lax.all_gather(proj_weight, "shard", axis=0, tiled=True),
        lax.all_gather(proj_bias, "shard", axis=0, tiled=True),
    )
    grad_inputs, grads, lefts, rights = backward(cotangent, filled, saved, gathered)
    parts = (
        lax.psum_scatter(
            grads[0].astype(jnp.bfloat16), "shard", scatter_dimension=0, tiled=True
        ).astype(jnp.float32),
        lax.psum_scatter(
            grads[1].astype(jnp.bfloat16), "shard", scatter_dimension=0, tiled=True
        ).astype(jnp.float32),
        lax.psum_scatter(
            grads[2].astype(jnp.bfloat16), "shard", scatter_dimension=0, tiled=True
        ).astype(jnp.float32),
        lax.psum_scatter(
            grads[3].astype(jnp.bfloat16), "shard", scatter_dimension=0, tiled=True
        ).astype(jnp.float32),
        lax.psum_scatter(
            grads[4].astype(jnp.bfloat16), "shard", scatter_dimension=0, tiled=True
        ).astype(jnp.float32),
        lax.psum_scatter(
            grads[5].astype(jnp.bfloat16), "shard", scatter_dimension=0, tiled=True
        ).astype(jnp.float32),
        lax.psum_scatter(
            grads[6].astype(jnp.bfloat16), "shard", scatter_dimension=0, tiled=True
        ).astype(jnp.float32),
        lax.psum_scatter(
            grads[7].astype(jnp.bfloat16), "shard", scatter_dimension=0, tiled=True
        ).astype(jnp.float32),
        lax.psum_scatter(
            grads[8].astype(jnp.bfloat16), "shard", scatter_dimension=0, tiled=True
        ).astype(jnp.float32),
        lax.psum_scatter(
            grads[9].astype(jnp.bfloat16), "shard", scatter_dimension=0, tiled=True
        ).astype(jnp.float32),
        lax.psum_scatter(
            grads[10].astype(jnp.bfloat16), "shard", scatter_dimension=0, tiled=True
        ).astype(jnp.float32),
        lax.psum_scatter(
            grads[11].astype(jnp.bfloat16), "shard", scatter_dimension=0, tiled=True
        ).astype(jnp.float32),
        lax.psum_scatter(
            grads[12].astype(jnp.bfloat16), "shard", scatter_dimension=0, tiled=True
        ).astype(jnp.float32),
    )
    totals = (
        lax.psum(parts[0].astype(jnp.bfloat16), "replica").astype(jnp.float32),
        lax.psum(parts[1].astype(jnp.bfloat16), "replica").astype(jnp.float32),
        lax.psum(parts[2].astype(jnp.bfloat16), "replica").astype(jnp.float32),
        lax.psum(parts[3].astype(jnp.bfloat16), "replica").astype(jnp.float32),
        lax.psum(parts[4].astype(jnp.bfloat16), "replica").astype(jnp.float32),
        lax.psum(parts[5].astype(jnp.bfloat16), "replica").astype(jnp.float32),
        lax.psum(parts[6].astype(jnp.bfloat16), "replica").astype(jnp.float32),
        lax.psum(parts[7].astype(jnp.bfloat16), "replica").astype(jnp.float32),
        lax.psum(parts[8].astype(jnp.bfloat16), "replica").astype(jnp.float32),
        lax.psum(parts[9].astype(jnp.bfloat16), "replica").astype(jnp.float32),
        lax.psum(parts[10].astype(jnp.bfloat16), "replica").astype(jnp.float32),
        lax.psum(parts[11].astype(jnp.bfloat16), "replica").astype(jnp.float32),
        lax.psum(parts[12].astype(jnp.bfloat16), "replica").astype(jnp.float32),
    )
    return (
        result,
        grad_inputs,
        totals[0],
        totals[1],
        totals[2],
        totals[3],
        totals[4],
        totals[5],
        totals[6],
        totals[7],
        totals[8],
        totals[9],
        totals[10],
        totals[11],
        totals[12],
    )


def solution(mesh):
    placed = (
        P(("shard", "replica"), None),
        P("shard"),
        P("shard"),
        P("shard", None),
        P("shard"),
        P("shard"),
        P("shard", None),
        P("shard"),
        P("shard"),
        P("shard"),
        P("shard", None),
        P("shard"),
        P("shard", None),
        P("shard"),
        P(("shard", "replica"), None),
        P(),
        P(),
        P(),
    )
    return jax.shard_map(
        local,
        mesh=mesh,
        in_specs=placed,
        out_specs=(
            P(("shard", "replica"), None),
            P(("shard", "replica"), None),
            P("shard"),
            P("shard"),
            P("shard", None),
            P("shard"),
            P("shard"),
            P("shard", None),
            P("shard"),
            P("shard"),
            P("shard"),
            P("shard", None),
            P("shard"),
            P("shard", None),
            P("shard"),
        ),
        check_vma=False,
    )
```

profile of v0, /device:TPU:0, one launch (start us, length us, event | category | flops | bytes accessed | tf_op | source)
XLA Modules:
  0.0 1449.5 jit_solution(5690311170459568473)
XLA Ops:
  14.2 14.2 all-reduce.21
  29.5 82.0 %all-gather.5.cloned.1.call-done = bf16[1600,4800]{1,0:T(8,128)(2,1)} async-done(((bf16[400,4800]{1,0:T(8,128)(2,1)}), bf16[1600,4800]{1,0:T(8,128)(2,1)}) %all-gather.5.cloned.1.call-update) | async-done | bytes 15360016 | tf_op jit(solution)/shard_map/all_gather | solution.py:270
  111.5 14.2 fusion.7
  134.2 19.9 %all-gather.7.cloned.1.call-done = bf16[1600,1600]{1,0:T(8,128)(2,1)} async-done(((bf16[400,1600]{1,0:T(8,128)(2,1)}), bf16[1600,1600]{1,0:T(8,128)(2,1)}) %all-gather.7.cloned.1.call-update) | async-done | bytes 5120016 | tf_op jit(solution)/shard_map/all_gather | solution.py:273
  154.0 4.9 fusion.78
  159.2 125.3 %all-gather.9.cloned.1.call-done = bf16[1600,6400]{1,0:T(8,128)(2,1)} async-done(((bf16[400,6400]{1,0:T(8,128)(2,1)}), bf16[1600,6400]{1,0:T(8,128)(2,1)}) %all-gather.9.cloned.1.call-update) | async-done | bytes 20480016 | tf_op jit(solution)/shard_map/all_gather | solution.py:277
  284.5 12.7 convolution_add_fusion
  297.2 122.2 %all-gather.11.cloned.1.call-done = bf16[6400,1600]{1,0:T(8,128)(2,1)} async-done(((bf16[1600,1600]{1,0:T(8,128)(2,1)}), bf16[6400,1600]{1,0:T(8,128)(2,1)}) %all-gather.11.cloned.1.call-update) | async-done | bytes 20480016 | tf_op jit(solution)/shard_map/all_gather | solution.py:279
  419.4 13.5 fusion.81
  432.9 13.1 multiply_reduce_fusion.1
  461.2 12.9 fusion.52
  474.1 13.4 bitcast_convert_fusion.1
  487.6 5.8 bitcast_convert_fusion
  493.4 12.1 convolution_convert_fusion.2
  505.6 16.7 %convolution_convert_fusion = bf16[6400,1600]{1,0:T(8,128)(2,1)} fusion(bf16[256,1600]{0,1:T(8,128)(2,1)} %param.32, pred[256]{0:T(512)(128)(4,1)S(1)} %fusion.63, f32[256,6400]{1,0:T(8,128)} %convolution_add_fusion), kind=kOutput, calls=%fused_computation.1 | convolution fusion | flops 5269094400 | bytes 27853056 | tf_op jit(solution)/shard_map/dot_general | solution.py:57
  522.3 12.6 convolution_convert_fusion.1
  535.0 90.8 %reduce-scatter.5.cloned.1.call-done = bf16[400,4800]{1,0:T(8,128)(2,1)} async-done(((bf16[1600,4800]{1,0:T(8,128)(2,1)}), bf16[400,4800]{1,0:T(8,128)(2,1)}) %reduce-scatter.5.cloned.1.call-update) | async-done | bytes 3840016 | tf_op jit(solution)/shard_map/reduce_scatter | solution.py:308
  625.8 155.1 %reduce-scatter.11.cloned.1.call-done = bf16[1600,1600]{1,0:T(8,128)(2,1)} async-done(((bf16[6400,1600]{1,0:T(8,128)(2,1)}), bf16[1600,1600]{1,0:T(8,128)(2,1)}) %reduce-scatter.11.cloned.1.call-update) | async-done | bytes 5120016 | tf_op jit(solution)/shard_map/reduce_scatter | solution.py:335
  781.0 158.1 %reduce-scatter.9.cloned.1.call-done = bf16[400,6400]{1,0:T(8,128)(2,1)} async-done(((bf16[1600,6400]{1,0:T(8,128)(2,1)}), bf16[400,6400]{1,0:T(8,128)(2,1)}) %reduce-scatter.9.cloned.1.call-update) | async-done | bytes 5120016 | tf_op jit(solution)/shard_map/reduce_scatter | solution.py:329
  944.3 13.3 fusion.44
  957.6 11.5 all-reduce.20
  969.8 39.6 %all-reduce.18 = (bf16[400]{0:T(512)(128)(2,1)S(1)}, bf16[400]{0:T(512)(128)(2,1)S(1)}, bf16[400]{0:T(512)(128)(2,1)S(1)}, bf16[400]{0:T(512)(128)(2,1)S(1)}, bf...) all-reduce(bf16[400]{0:T(512)(128)(2,1)S(1)} %dynamic-slice.10, ...), channel_id=1, replica_groups=mesh['shard'=4,'replica'=8] {'replica'}, use_global_device_ids=true, to_apply=%region_15.16 | all-reduce | flops 4800 | bytes 19200 | tf_op jit(solution)/shard_map/psum | solution.py:343
  1017.8 17.3 %fusion.30 = bf16[256,1600]{0,1:T(8,128)(2,1)} fusion(f32[256,1600]{0,1:T(8,128)S(1)} %get-tuple-element.65, bf16[6400,1600]{1,0:T(8,128)(2,1)} %all-gather.11.cloned.1.call-done, f32[1600]{0:T(1024)S(1)} %convert_element_type.211, f32[256,6400]{1,0:T(8,128)} %convolution_add_fusion), kind=kOutput, calls=%fused_computation.39 | convolution fusion | flops 5258854400 | bytes 29497600 | tf_op jit(solution)/shard_map/dot_general | solution.py:53
  1035.1 389.8 %all-reduce.24.cloned.1.call-done = (bf16[400,4800]{1,0:T(8,128)(2,1)}, bf16[400,1600]{1,0:T(8,128)(2,1)}, bf16[400,6400]{1,0:T(8,128)(2,1)}, bf16[1600,1600]{1,0:T(8,128)(2,1)}) async-done(((bf16[400,4800]{1,0:T(8,128)(2,1)}, bf16[400,1600]{1,0:T(8,128)(2,1)}, bf16[400,6400]{1,0:T(8,128)(2,1)}, bf16[1600,1600]{1,0:T(8,128)(2,1)}), (bf16[400,4800]{1,0:T(8,128)(2,1)}, bf16[400,1600]{1,0:T(8,128)(2,1)}, ...) | async-done | bytes 15360016 | tf_op jit(solution)/shard_map/psum | solution.py:345
  (156 shorter events, 61.0 us)
Async XLA Ops:
  7.2 104.3 %all-gather.5.cloned.1.call-start = ((), (), s32[]{:S(2)}) async-start(), calls=%async_computation.4 | async-start | bytes 19456000 | tf_op jit(solution)/shard_map/all_gather | solution.py:270
  7.9 146.1 %all-gather.7.cloned.1.call-start = ((), (), s32[]{:S(2)}) async-start(), calls=%async_computation.5 | async-start | bytes 6656000 | tf_op jit(solution)/shard_map/all_gather | solution.py:273
  8.7 4.4 copy-start.20
  8.7 4.6 copy-start.21
  8.7 4.9 copy-start.22
  8.8 5.1 copy-start.13
  8.8 19.7 %copy-start.15 = (s32[128]{0:T(128)S(1)}, s32[128]{0:T(128)}, u32[]{:S(2)}) copy-start(s32[128]{0:T(128)} %param.35) | copy-start | bytes 1540
  8.8 19.7 %copy-start.24 = (s32[128]{0:T(128)S(1)}, s32[128]{0:T(128)}, u32[]{:S(2)}) copy-start(s32[128]{0:T(128)} %param.33) | copy-start | bytes 1540
  8.8 19.8 %copy-start.25 = (s32[128]{0:T(128)S(1)}, s32[128]{0:T(128)}, u32[]{:S(2)}) copy-start(s32[128]{0:T(128)} %param.34) | copy-start | bytes 1540
  8.8 20.0 %copy-start.1 = (bf16[256,1600]{0,1:T(8,128)(2,1)S(1)}, bf16[256,1600]{0,1:T(8,128)(2,1)}, u32[]{:S(2)}) copy-start(bf16[256,1600]{0,1:T(8,128)(2,1)} %param.18) | copy-start | bytes 2457604
  8.8 275.7 %all-gather.9.cloned.1.call-start = ((), (), s32[]{:S(2)}) async-start(), calls=%async_computation.6 | async-start | bytes 25600000 | tf_op jit(solution)/shard_map/all_gather | solution.py:277
  9.5 409.8 %all-gather.11.cloned.1.call-start = ((), (), s32[]{:S(2)}) async-start(), calls=%async_computation.7 | async-start | bytes 26624000 | tf_op jit(solution)/shard_map/all_gather | solution.py:279
  10.1 524.9 %reduce-scatter.7.cloned.1.call-start = ((), (), s32[]{:S(2)}) async-start(), calls=%async_computation.9 | async-start | bytes 6656000 | tf_op jit(solution)/shard_map/reduce_scatter | solution.py:317
  134.2 24.8 %copy-start.9 = (bf16[25,64,256]{2,1,0:T(8,128)(2,1)}, bf16[25,64,256]{2,1,0:T(8,128)(2,1)S(1)}, u32[]{:S(2)}) copy-start(bf16[25,64,256]{2,1,0:T(8,128)(2,1)S(1)} %fusion.51) | copy-start | bytes 2457604
  159.2 260.2 %copy-start.11 = (bf16[256,1600]{0,1:T(8,128)(2,1)S(1)}, bf16[256,1600]{0,1:T(8,128)(2,1)}, u32[]{:S(2)}) copy-start(bf16[256,1600]{0,1:T(8,128)(2,1)} %param.32) | copy-start | bytes 2457604
  432.9 13.2 copy-start.12
  451.2 174.6 %reduce-scatter.5.cloned.1.call-start = ((), (), s32[]{:S(2)}) async-start(), calls=%async_computation.8 | async-start | bytes 19456000 | tf_op jit(solution)/shard_map/reduce_scatter | solution.py:308
  451.5 5.2 copy-start.7
  505.5 275.5 %reduce-scatter.11.cloned.1.call-start = ((), (), s32[]{:S(2)}) async-start(), calls=%async_computation.11 | async-start | bytes 26624000 | tf_op jit(solution)/shard_map/reduce_scatter | solution.py:335
  522.3 416.8 %reduce-scatter.9.cloned.1.call-start = ((), (), s32[]{:S(2)}) async-start(), calls=%async_computation.10 | async-start | bytes 25600000 | tf_op jit(solution)/shard_map/reduce_scatter | solution.py:329
  534.9 889.9 %all-reduce.24.cloned.1.call-start = ((), (), s32[]{:S(2)}) async-start(), calls=%async_computation.12 | async-start | bytes 31334400 | tf_op jit(solution)/shard_map/psum | solution.py:345
  1428.0 4.9 copy-start.2
  1428.0 9.6 slice-start
  1433.0 4.7 slice-start.1
  (13 other events, 32.3 us)
Sparse Core Ops, SparseCore 0:
  9.6 101.8 all-gather.4
  113.0 40.9 all-gather.6
  155.6 128.8 all-gather.8
  285.9 133.3 all-gather.10
  451.4 51.8 reduce-scatter.6
  505.8 119.9 reduce-scatter.4
  628.4 152.4 reduce-scatter.10
  783.6 155.4 reduce-scatter.8
  943.8 481.0 all-reduce.23
where the time goes:
time: 1450 us
  waiting for transfers between devices  1150 us (79%)
  matrix products  178 us (12%)
  blocking collectives  65.2 us (4%)
  other arithmetic  32.3 us (2%)
  between operations  17.4 us (1%)
    psum x1, waiting for transfers between devices, local(): lax.psum(parts[2].astype(jnp.bfloat16), 'replica').astype(jnp.float32)  390 us
    reduce_scatter x1, waiting for transfers between devices, local(): lax.psum_scatter(grads[9].astype(jnp.bfloat16), 'shard', scatter_dimensio...  158 us
    reduce_scatter x1, waiting for transfers between devices, local(): lax.psum_scatter(grads[11].astype(jnp.bfloat16), 'shard', scatter_dimensi...  155 us
    all_gather x1, waiting for transfers between devices, local(): lax.all_gather(fc_weight, 'shard', axis=0, tiled=True)  125 us
    all_gather x1, waiting for transfers between devices, local(): lax.all_gather(proj_weight, 'shard', axis=0, tiled=True)  122 us
    reduce_scatter x1, waiting for transfers between devices, local(): lax.psum_scatter(grads[2].astype(jnp.bfloat16), 'shard', scatter_dimensio...  90.8 us
    all_gather x1, waiting for transfers between devices, local(): lax.all_gather(qkv_weight, 'shard', axis=0, tiled=True)  82 us
    dot_general x4, matrix products, mdot(): return jnp.dot(left, right, preferred_element_type=jnp.float32)  49.2 us
  transfers between devices with their start and end apart: 9, of which 8 were waited for; matrix products, arithmetic and copies ran while one was open for 12% of the time, Pallas kernels for 0%

commit v1 on v0

--- a/solution.py
+++ b/solution.py
@@ -6,6 +6,12 @@
 
 HEAD = 64
 GELU_C = math.sqrt(2.0 / math.pi)
+
+
+def add_all(x, name):
+    parts = lax.all_gather(x, name, axis=0, tiled=False)
+    total = parts.sum(axis=0)
+    return total
 
 
 def normalize(values):
@@ -342,7 +348,7 @@
     totals = (
         lax.psum(parts[0].astype(jnp.bfloat16), "replica").astype(jnp.float32),
         lax.psum(parts[1].astype(jnp.bfloat16), "replica").astype(jnp.float32),
-        lax.psum(parts[2].astype(jnp.bfloat16), "replica").astype(jnp.float32),
+        add_all(parts[2].astype(jnp.bfloat16), "replica").astype(jnp.float32),
         lax.psum(parts[3].astype(jnp.bfloat16), "replica").astype(jnp.float32),
         lax.psum(parts[4].astype(jnp.bfloat16), "replica").astype(jnp.float32),
         lax.psum(parts[5].astype(jnp.bfloat16), "replica").astype(jnp.float32),

time: 1450 us -> 1930 us (1.33)
  waiting for transfers between devices: 1150 us -> 1600 us
    all_gather x0 -> x1, waiting for transfers between devices: none -> 577 us  [add_all(): parts = lax.all_gather(x, name, axis=0, tiled=False)]
    psum x1, waiting for transfers between devices: 390 us -> 271 us  [local(): lax.psum(parts[5].astype(jnp.bfloat16), 'replica').astype(jnp.float32)]
    reduce_scatter x1, waiting for transfers between devices: 155 us -> 122 us  [local(): lax.psum_scatter(grads[11].astype(jnp.bfloat16), 'shard', scatter_dimensi...]
    reduce_scatter x1, waiting for transfers between devices: 90.8 us -> 122 us  [local(): lax.psum_scatter(grads[2].astype(jnp.bfloat16), 'shard', scatter_dimensio...]
  transfers between devices with their start and end apart: 9 -> 10, of which waited for: 8 -> 9; matrix products, arithmetic and copies ran while one was open for 12% -> 10% of each run, Pallas kernels for 0% -> 0%
where the time goes in v1:
time: 1930 us; the launch traced here: 1920 us
  waiting for transfers between devices  1600 us (83%)
  matrix products  180 us (9%)
  blocking collectives  65.2 us (3%)
  other arithmetic  50 us (3%)
    all_gather x1, waiting for transfers between devices, add_all(): parts = lax.all_gather(x, name, axis=0, tiled=False)  577 us
    psum x1, waiting for transfers between devices, local(): lax.psum(parts[5].astype(jnp.bfloat16), 'replica').astype(jnp.float32)  271 us
    reduce_scatter x1, waiting for transfers between devices, local(): lax.psum_scatter(grads[9].astype(jnp.bfloat16), 'shard', scatter_dimensio...  158 us
    all_gather x1, waiting for transfers between devices, local(): lax.all_gather(fc_weight, 'shard', axis=0, tiled=True)  125 us
    reduce_scatter x1, waiting for transfers between devices, local(): lax.psum_scatter(grads[2].astype(jnp.bfloat16), 'shard', scatter_dimensio...  122 us
    reduce_scatter x1, waiting for transfers between devices, local(): lax.psum_scatter(grads[11].astype(jnp.bfloat16), 'shard', scatter_dimensi...  122 us
    all_gather x1, waiting for transfers between devices, local(): lax.all_gather(proj_weight, 'shard', axis=0, tiled=True)  122 us
    all_gather x1, waiting for transfers between devices, local(): lax.all_gather(qkv_weight, 'shard', axis=0, tiled=True)  81.9 us
  transfers between devices with their start and end apart: 10, of which 9 were waited for; matrix products, arithmetic and copies ran while one was open for 10% of the time, Pallas kernels for 0%

profile of v1, /device:TPU:0, one launch (start us, length us, event | category | flops | bytes accessed | tf_op | source)
XLA Modules:
  0.0 1924.9 jit_solution(8266711582846910500)
XLA Ops:
  14.2 14.2 all-reduce.21
  29.6 81.9 %all-gather.7.cloned.1.call-done = bf16[1600,4800]{1,0:T(8,128)(2,1)} async-done(((bf16[400,4800]{1,0:T(8,128)(2,1)}), bf16[1600,4800]{1,0:T(8,128)(2,1)}) %all-gather.7.cloned.1.call-update) | async-done | bytes 15360016 | tf_op jit(solution)/shard_map/all_gather | solution.py:276
  111.5 14.2 fusion.7
  134.2 19.8 %all-gather.9.cloned.1.call-done = bf16[1600,1600]{1,0:T(8,128)(2,1)} async-done(((bf16[400,1600]{1,0:T(8,128)(2,1)}), bf16[1600,1600]{1,0:T(8,128)(2,1)}) %all-gather.9.cloned.1.call-update) | async-done | bytes 5120016 | tf_op jit(solution)/shard_map/all_gather | solution.py:279
  159.2 125.3 %all-gather.11.cloned.1.call-done = bf16[1600,6400]{1,0:T(8,128)(2,1)} async-done(((bf16[400,6400]{1,0:T(8,128)(2,1)}), bf16[1600,6400]{1,0:T(8,128)(2,1)}) %all-gather.11.cloned.1.call-update) | async-done | bytes 20480016 | tf_op jit(solution)/shard_map/all_gather | solution.py:283
  284.5 12.7 convolution_add_fusion
  297.2 122.1 %all-gather.13.cloned.1.call-done = bf16[6400,1600]{1,0:T(8,128)(2,1)} async-done(((bf16[1600,1600]{1,0:T(8,128)(2,1)}), bf16[6400,1600]{1,0:T(8,128)(2,1)}) %all-gather.13.cloned.1.call-update) | async-done | bytes 20480016 | tf_op jit(solution)/shard_map/all_gather | solution.py:285
  419.4 13.5 fusion.81
  432.9 13.3 multiply_reduce_fusion.1
  451.5 14.5 convolution_convert_fusion
  466.1 12.2 convolution_convert_fusion.1
  487.6 12.9 fusion.52
  500.5 13.3 bitcast_convert_fusion.1
  522.2 13.9 convolution_convert_fusion.2
  536.2 122.2 %reduce-scatter.11.cloned.1.call-done = bf16[1600,1600]{1,0:T(8,128)(2,1)} async-done(((bf16[6400,1600]{1,0:T(8,128)(2,1)}), bf16[1600,1600]{1,0:T(8,128)(2,1)}) %reduce-scatter.11.cloned.1.call-update) | async-done | bytes 5120016 | tf_op jit(solution)/shard_map/reduce_scatter | solution.py:341
  658.4 158.1 %reduce-scatter.9.cloned.1.call-done = bf16[400,6400]{1,0:T(8,128)(2,1)} async-done(((bf16[1600,6400]{1,0:T(8,128)(2,1)}), bf16[400,6400]{1,0:T(8,128)(2,1)}) %reduce-scatter.9.cloned.1.call-update) | async-done | bytes 5120016 | tf_op jit(solution)/shard_map/reduce_scatter | solution.py:335
  816.6 122.5 %reduce-scatter.5.cloned.1.call-done = bf16[400,4800]{1,0:T(8,128)(2,1)} async-done(((bf16[1600,4800]{1,0:T(8,128)(2,1)}), bf16[400,4800]{1,0:T(8,128)(2,1)}) %reduce-scatter.5.cloned.1.call-update) | async-done | bytes 3840016 | tf_op jit(solution)/shard_map/reduce_scatter | solution.py:314
  944.3 13.5 fusion.44
  957.8 11.5 all-reduce.20
  970.0 39.5 %all-reduce.18 = (bf16[400]{0:T(512)(128)(2,1)S(1)}, bf16[400]{0:T(512)(128)(2,1)S(1)}, bf16[400]{0:T(512)(128)(2,1)S(1)}, bf16[400]{0:T(512)(128)(2,1)S(1)}, bf...) all-reduce(bf16[400]{0:T(512)(128)(2,1)S(1)} %dynamic-slice.10, ...), channel_id=1, replica_groups=mesh['shard'=4,'replica'=8] {'replica'}, use_global_device_ids=true, to_apply=%region_15.16 | all-reduce | flops 4800 | bytes 19200 | tf_op jit(solution)/shard_map/psum | solution.py:349
  1017.8 17.6 fusion.30
  1035.4 270.6 %all-reduce.24.cloned.1.call-done = (bf16[400,1600]{1,0:T(8,128)(2,1)}, bf16[400,6400]{1,0:T(8,128)(2,1)}, bf16[1600,1600]{1,0:T(8,128)(2,1)}) async-done(((bf16[400,1600]{1,0:T(8,128)(2,1)}, bf16[400,6400]{1,0:T(8,128)(2,1)}, bf16[1600,1600]{1,0:T(8,128)(2,1)}), (bf16[400,1600]{1,0:T(8,128)(2,1)}, bf16[400,6400]{1,0:T(8,128)(2,1)}, bf16[1600,1600]{1,0:T(8,128)(2,1)})) %all-reduce.24.cloned.1.call-update) | async-done | bytes 11520016 | tf_op jit(solution)/shard_map/psum | solution.py:354
  1321.7 576.9 %all-gather.15.cloned.1.call-done = bf16[3200,4800]{1,0:T(8,128)(2,1)} async-done(((bf16[400,4800]{1,0:T(8,128)(2,1)}), bf16[3200,4800]{1,0:T(8,128)(2,1)}) %all-gather.15.cloned.1.call-update) | async-done | bytes 30720016 | tf_op jit(solution)/shard_map/all_gather | solution.py:12
  1898.6 13.4 reduce_sum.205
  (156 shorter events, 77.6 us)
Async XLA Ops:
  7.2 104.3 %all-gather.7.cloned.1.call-start = ((), (), s32[]{:S(2)}) async-start(), calls=%async_computation.4 | async-start | bytes 19456000 | tf_op jit(solution)/shard_map/all_gather | solution.py:276
  7.9 146.1 %all-gather.9.cloned.1.call-start = ((), (), s32[]{:S(2)}) async-start(), calls=%async_computation.5 | async-start | bytes 6656000 | tf_op jit(solution)/shard_map/all_gather | solution.py:279
  8.7 4.6 copy-start.19
  8.7 4.9 copy-start.20
  8.8 5.1 copy-start.11
  8.8 19.7 %copy-start.13 = (s32[128]{0:T(128)S(1)}, s32[128]{0:T(128)}, u32[]{:S(2)}) copy-start(s32[128]{0:T(128)} %param.35) | copy-start | bytes 1540
  8.8 19.7 %copy-start.22 = (s32[128]{0:T(128)S(1)}, s32[128]{0:T(128)}, u32[]{:S(2)}) copy-start(s32[128]{0:T(128)} %param.33) | copy-start | bytes 1540
  8.8 19.8 %copy-start.23 = (s32[128]{0:T(128)S(1)}, s32[128]{0:T(128)}, u32[]{:S(2)}) copy-start(s32[128]{0:T(128)} %param.34) | copy-start | bytes 1540
  8.8 20.1 %copy-start.1 = (bf16[256,1600]{0,1:T(8,128)(2,1)S(1)}, bf16[256,1600]{0,1:T(8,128)(2,1)}, u32[]{:S(2)}) copy-start(bf16[256,1600]{0,1:T(8,128)(2,1)} %param.18) | copy-start | bytes 2457604
  8.8 275.7 %all-gather.11.cloned.1.call-start = ((), (), s32[]{:S(2)}) async-start(), calls=%async_computation.6 | async-start | bytes 25600000 | tf_op jit(solution)/shard_map/all_gather | solution.py:283
  9.5 409.8 %all-gather.13.cloned.1.call-start = ((), (), s32[]{:S(2)}) async-start(), calls=%async_computation.7 | async-start | bytes 26624000 | tf_op jit(solution)/shard_map/all_gather | solution.py:285
  10.1 526.1 %reduce-scatter.7.cloned.1.call-start = ((), (), s32[]{:S(2)}) async-start(), calls=%async_computation.9 | async-start | bytes 6656000 | tf_op jit(solution)/shard_map/reduce_scatter | solution.py:323
  134.2 24.7 %copy-start.7 = (bf16[25,64,256]{2,1,0:T(8,128)(2,1)}, bf16[25,64,256]{2,1,0:T(8,128)(2,1)S(1)}, u32[]{:S(2)}) copy-start(bf16[25,64,256]{2,1,0:T(8,128)(2,1)S(1)} %fusion.51) | copy-start | bytes 2457604
  159.2 260.2 %copy-start.9 = (bf16[256,1600]{0,1:T(8,128)(2,1)S(1)}, bf16[256,1600]{0,1:T(8,128)(2,1)}, u32[]{:S(2)}) copy-start(bf16[256,1600]{0,1:T(8,128)(2,1)} %param.32) | copy-start | bytes 2457604
  432.9 13.3 copy-start.10
  451.4 207.0 %reduce-scatter.11.cloned.1.call-start = ((), (), s32[]{:S(2)}) async-start(), calls=%async_computation.11 | async-start | bytes 26624000 | tf_op jit(solution)/shard_map/reduce_scatter | solution.py:341
  466.0 350.5 %reduce-scatter.9.cloned.1.call-start = ((), (), s32[]{:S(2)}) async-start(), calls=%async_computation.10 | async-start | bytes 25600000 | tf_op jit(solution)/shard_map/reduce_scatter | solution.py:335
  478.3 460.8 %reduce-scatter.5.cloned.1.call-start = ((), (), s32[]{:S(2)}) async-start(), calls=%async_computation.8 | async-start | bytes 19456000 | tf_op jit(solution)/shard_map/reduce_scatter | solution.py:314
  478.6 5.1 copy-start.5
  536.1 769.9 %all-reduce.24.cloned.1.call-start = ((), (), s32[]{:S(2)}) async-start(), calls=%async_computation.13 | async-start | bytes 23552000 | tf_op jit(solution)/shard_map/psum | solution.py:354
  816.5 123.9 %copy-start.21 = (bf16[400]{0:T(512)(128)(2,1)S(1)}, bf16[400]{0:T(512)(128)(2,1)}, u32[]{:S(2)}) copy-start(bf16[400]{0:T(512)(128)(2,1)} %param.31) | copy-start | bytes 2404
  816.6 1082.1 %all-gather.15.cloned.1.call-start = ((), (), s32[]{:S(2)}) async-start(), calls=%async_computation.12 | async-start | bytes 35020800 | tf_op jit(solution)/shard_map/all_gather | solution.py:12
  1306.0 10.8 slice-start
  1309.2 7.7 slice-start.1
  (12 other events, 32.3 us)
Sparse Core Ops, SparseCore 0:
  9.5 101.8 all-gather.6
  113.0 40.9 all-gather.8
  155.6 128.8 all-gather.10
  285.9 133.3 all-gather.12
  451.5 51.8 reduce-scatter.6
  505.9 152.4 reduce-scatter.10
  661.0 155.4 reduce-scatter.8
  819.2 119.8 reduce-scatter.4
  943.5 362.5 all-reduce.23
  1307.4 591.1 all-gather.14
